TPU v7x, 32 devices: a whole 2x2x4 slice. The times are simulated.
32 devices in a mesh: dp: 8 (over z, x), seq: 4 (over y, core).
Axes of the slice: x: 2, y: 2, z: 4, core: 2. Of those that a mesh axis runs over, the one named last changes fastest.
Arguments:
- tokens: bfloat16 [16384, 1024], P(('dp', 'seq')), may hold values from -6 to 6
- time_embed: bfloat16 [32, 1024], P(('dp', 'seq')), may hold values from -6 to 6
- lengths: int32 [32], P('dp'), may hold values from 0 to 475, as said below
- cotangent: bfloat16 [16384, 1024], P(('dp', 'seq')), may hold values from -6 to 6
- w_query: bfloat16 [1024, 1024], P('seq'), may hold values from -0.1875 to 0.1875
- w_key: bfloat16 [1024, 1024], P('seq'), may hold values from -0.1875 to 0.1875
- w_value: bfloat16 [1024, 1024], P('seq'), may hold values from -0.1875 to 0.1875
- w_out: bfloat16 [1024, 1024], P('seq'), may hold values from -0.75 to 0.75
- w_time: bfloat16 [1024, 1024], P('seq'), may hold values from -0.1875 to 0.1875
- w_in: bfloat16 [4096, 1024], P('seq'), may hold values from -0.1875 to 0.1875
- w_down: bfloat16 [4096, 1024], P('seq'), may hold values from -0.09375 to 0.09375
- b_query: bfloat16 [1024], replicated, may hold values from -3 to 3
- b_value: bfloat16 [1024], replicated, may hold values from -3 to 3
- b_out: bfloat16 [1024], replicated, may hold values from -3 to 3
- b_time: bfloat16 [1024], replicated, may hold values from -3 to 3
- b_in: bfloat16 [4096], replicated, may hold values from -3 to 3
- b_down: bfloat16 [1024], replicated, may hold values from -2 to 2
- gain_one: bfloat16 [1024], replicated, may hold values from 0.25 to 1.75
- shift_one: bfloat16 [1024], replicated, may hold values from -2 to 2
- gain_two: bfloat16 [1024], replicated, may hold values from 0.25 to 1.75
- shift_two: bfloat16 [1024], replicated, may hold values from -2 to 2
Outputs:
- layer_out: bfloat16 [16384, 1024], P(('dp', 'seq'))
- grad_tokens: bfloat16 [16384, 1024], P(('dp', 'seq'))
- grad_w_query: float32 [1024, 1024], P('seq')
- grad_w_key: float32 [1024, 1024], P('seq')
- grad_w_value: float32 [1024, 1024], P('seq')
- grad_w_out: float32 [1024, 1024], P('seq')
- grad_w_time: float32 [1024, 1024], P('seq')
- grad_w_in: float32 [4096, 1024], P('seq')
- grad_w_down: float32 [4096, 1024], P('seq')
- grad_b_query: float32 [1024], replicated
- grad_b_value: float32 [1024], replicated
- grad_b_out: float32 [1024], replicated
- grad_b_time: float32 [1024], replicated
- grad_b_in: float32 [4096], replicated
- grad_b_down: float32 [1024], replicated
- grad_gain_one: float32 [1024], replicated
- grad_shift_one: float32 [1024], replicated
- grad_gain_two: float32 [1024], replicated
- grad_shift_two: float32 [1024], replicated
Inputs may be any that keep to these rules, and one draw needn't show every extreme that they name: Item i's valid slots are its first lengths[i] + 25; every draw has an item of length 475 and one of length 0.
All inputs are finite; a program needn't handle non-finite values.
Results may differ from a plain program's by a relative error of at most 0.02.
Values may be sent and summed in bfloat16 or wider, within the bound.
A program may use at most 256 MiB of HBM per device.

v0:
```python
import jax
import jax.numpy as jnp
from jax import lax
from jax.sharding import PartitionSpec as P

HEAD_DIM = 64
BLOCK = 25
norm_eps = 1e-05
neg_large = -1e30


def layer_norm(values, gain, shift):
    center = values - jnp.mean(values, axis=-1, keepdims=True)
    spread = lax.rsqrt(jnp.mean(center * center, axis=-1, keepdims=True) + norm_eps)
    return center * spread * gain + shift


def exact_gelu(values):
    return jax.nn.gelu(values, approximate=False)


def split_heads(rows):
    return rows.reshape(rows.shape[0], rows.shape[1] // HEAD_DIM, HEAD_DIM)


def item_scores(item_block, key_valid):
    queries = split_heads(item_block[:, 0])
    key_heads = split_heads(item_block[:, 1])
    value_heads = split_heads(item_block[:, 2])
    scores = jnp.einsum(
        "qhd,khd->hqk", queries, key_heads, preferred_element_type=jnp.float32
    ) * HEAD_DIM ** (-0.5)
    masked = jnp.where(key_valid[None, None, :], scores, neg_large)
    return (queries, key_heads, value_heads, masked)


def attend_forward(packed):
    item_block, key_valid = packed
    queries, key_heads, value_heads, masked = item_scores(item_block, key_valid)
    row_max = jnp.max(masked, axis=-1, keepdims=True)
    exp_scores = jnp.exp(masked - row_max)
    row_total = jnp.sum(exp_scores, axis=-1, keepdims=True)
    soft_weights = (exp_scores / row_total).astype(jnp.bfloat16)
    mixed_heads = jnp.einsum(
        "hqk,khd->qhd", soft_weights, value_heads, preferred_element_type=jnp.float32
    )
    log_total = row_max[:, :, 0] + jnp.log(row_total[:, :, 0])
    return (mixed_heads.reshape(item_block.shape[0], -1).astype(jnp.bfloat16), log_total)


def attend_backward(packed):
    item_block, key_valid, log_total, grad_block = packed
    queries, key_heads, value_heads, masked = item_scores(item_block, key_valid)
    soft_weights = jnp.exp(masked - log_total[:, :, None])
    grad_heads = split_heads(grad_block)
    grad_value = jnp.einsum(
        "hqk,qhd->khd",
        soft_weights.astype(jnp.bfloat16),
        grad_heads,
        preferred_element_type=jnp.float32,
    )
    grad_soft = jnp.einsum(
        "qhd,khd->hqk", grad_heads, value_heads, preferred_element_type=jnp.float32
    )
    grad_scores = soft_weights * (
        grad_soft - jnp.sum(soft_weights * grad_soft, axis=-1, keepdims=True)
    )
    scores_low = grad_scores.astype(jnp.bfloat16)
    score_scale = HEAD_DIM ** (-0.5)
    grad_query = (
        jnp.einsum("hqk,khd->qhd", scores_low, key_heads, preferred_element_type=jnp.float32)
        * score_scale
    )
    grad_key = (
        jnp.einsum("hqk,qhd->khd", scores_low, queries, preferred_element_type=jnp.float32)
        * score_scale
    )
    slot_count = item_block.shape[0]
    return jnp.stack(
        [
            grad_query.reshape(slot_count, -1),
            grad_key.reshape(slot_count, -1),
            grad_value.reshape(slot_count, -1),
        ],
        axis=1,
    ).astype(jnp.bfloat16)


def local(
    tokens,
    time_embed,
    lengths,
    cotangent,
    w_query,
    w_key,
    w_value,
    w_out,
    w_time,
    w_in,
    w_down,
    b_query,
    b_value,
    b_out,
    b_time,
    b_in,
    b_down,
    gain_one,
    shift_one,
    gain_two,
    shift_two,
):
    seq_rank = lax.axis_index("seq")
    item_count = time_embed.shape[0]
    token_count = tokens.shape[0]
    slot_count = token_count // item_count
    model_width = tokens.shape[1]
    full_query, full_key, full_value, full_out, full_time, full_in, full_down = (
        lax.all_gather(w_query, "seq", axis=0, tiled=True),
        lax.all_gather(w_key, "seq", axis=0, tiled=True),
        lax.all_gather(w_value, "seq", axis=0, tiled=True),
        lax.all_gather(w_out, "seq", axis=0, tiled=True),
        lax.all_gather(w_time, "seq", axis=0, tiled=True),
        lax.all_gather(w_in, "seq", axis=0, tiled=True),
        lax.all_gather(w_down, "seq", axis=0, tiled=True),
    )
    bias_query = b_query.astype(jnp.float32)
    bias_value = b_value.astype(jnp.float32)
    bias_out = b_out.astype(jnp.float32)
    bias_time = b_time.astype(jnp.float32)
    bias_in = b_in.astype(jnp.float32)
    bias_down = b_down.astype(jnp.float32)
    gain_first = gain_one.astype(jnp.float32)
    shift_first = shift_one.astype(jnp.float32)
    gain_last = gain_two.astype(jnp.float32)
    shift_last = shift_two.astype(jnp.float32)
    slot_index = lax.broadcasted_iota(jnp.int32, (lengths.shape[0], slot_count), 1)
    group_valid = slot_index < lengths[:, None] + BLOCK
    own_valid = lax.dynamic_slice_in_dim(group_valid, seq_rank * item_count, item_count, 0)
    row_keep = own_valid.reshape(token_count, 1).astype(jnp.float32)
    time_proj = jnp.dot(time_embed, full_time, preferred_element_type=jnp.float32) + bias_time
    resid = (tokens.reshape(item_count, slot_count, model_width) + time_proj[:, None, :]).reshape(
        token_count, model_width
    )
    resid_low = resid.astype(jnp.bfloat16)
    query_rows = (
        jnp.dot(resid_low, full_query, preferred_element_type=jnp.float32) + bias_query
    ).astype(jnp.bfloat16)
    key_rows = jnp.dot(resid_low, full_key, preferred_element_type=jnp.float32).astype(jnp.bfloat16)
    value_rows = (
        jnp.dot(resid_low, full_value, preferred_element_type=jnp.float32) + bias_value
    ).astype(jnp.bfloat16)
    stacked = jnp.stack([query_rows, key_rows, value_rows], axis=1).reshape(
        item_count, slot_count, 3, model_width
    )
    head_side = lax.all_to_all(stacked, "seq", split_axis=3, concat_axis=0, tiled=True)
    mixed_heads, log_totals = lax.map(attend_forward, (head_side, group_valid))
    mixed_rows = lax.all_to_all(
        mixed_heads, "seq", split_axis=0, concat_axis=2, tiled=True
    ).reshape(token_count, model_width)
    attn_out = jnp.dot(mixed_rows, full_out, preferred_element_type=jnp.float32) + bias_out
    first_norm, first_pull = jax.vjp(layer_norm, resid + attn_out, gain_first, shift_first)
    first_low = first_norm.astype(jnp.bfloat16)
    hidden_pre = (
        jnp.einsum("td,fd->tf", first_low, full_in, preferred_element_type=jnp.float32) + bias_in
    )
    hidden, gelu_pull = jax.vjp(exact_gelu, hidden_pre)
    hidden_low = hidden.astype(jnp.bfloat16)
    ffn_out = jnp.dot(hidden_low, full_down, preferred_element_type=jnp.float32) + bias_down
    second_norm, second_pull = jax.vjp(layer_norm, first_norm + ffn_out, gain_last, shift_last)
    layer_out = (second_norm * row_keep).astype(jnp.bfloat16)
    back_query, back_key, back_value, back_out, back_in, back_down = (
        lax.all_gather(w_query, "seq", axis=0, tiled=True),
        lax.all_gather(w_key, "seq", axis=0, tiled=True),
        lax.all_gather(w_value, "seq", axis=0, tiled=True),
        lax.all_gather(w_out, "seq", axis=0, tiled=True),
        lax.all_gather(w_in, "seq", axis=0, tiled=True),
        lax.all_gather(w_down, "seq", axis=0, tiled=True),
    )
    grad_second_in, grad_gain_two, grad_shift_two = second_pull(
        cotangent.astype(jnp.float32) * row_keep
    )
    grad_ffn = grad_second_in.astype(jnp.bfloat16)
    grad_hidden = jnp.einsum("td,fd->tf", grad_ffn, back_down, preferred_element_type=jnp.float32)
    grad_pre = gelu_pull(grad_hidden)[0].astype(jnp.bfloat16)
    grad_first = grad_second_in + jnp.dot(grad_pre, back_in, preferred_element_type=jnp.float32)
    grad_first_in, grad_gain_one, grad_shift_one = first_pull(grad_first)
    grad_attn = grad_first_in.astype(jnp.bfloat16)
    grad_mixed = jnp.einsum(
        "td,ed->te", grad_attn, back_out, preferred_element_type=jnp.float32
    ).astype(jnp.bfloat16)
    grad_heads = lax.all_to_all(
        grad_mixed.reshape(item_count, slot_count, model_width),
        "seq",
        split_axis=2,
        concat_axis=0,
        tiled=True,
    )
    grad_stack = lax.map(attend_backward, (head_side, group_valid, log_totals, grad_heads))
    grad_qkv = lax.all_to_all(grad_stack, "seq", split_axis=0, concat_axis=3, tiled=True).reshape(
        token_count, 3, model_width
    )
    grad_query_rows = grad_qkv[:, 0]
    grad_key_rows = grad_qkv[:, 1]
    grad_value_rows = grad_qkv[:, 2]
    grad_resid = grad_first_in + jnp.einsum(
        "te,de->td", grad_query_rows, back_query, preferred_element_type=jnp.float32
    )
    grad_resid = grad_resid + jnp.einsum(
        "te,de->td", grad_key_rows, back_key, preferred_element_type=jnp.float32
    )
    grad_resid = grad_resid + jnp.einsum(
        "te,de->td", grad_value_rows, back_value, preferred_element_type=jnp.float32
    )
    grad_tokens = grad_resid.astype(jnp.bfloat16)
    grad_time = jnp.sum(grad_resid.reshape(item_count, slot_count, model_width), axis=1).astype(
        jnp.bfloat16
    )
    term_in = jnp.einsum("tf,td->fd", grad_pre, first_low, preferred_element_type=jnp.float32)
    term_down = jnp.einsum("tf,td->fd", hidden_low, grad_ffn, preferred_element_type=jnp.float32)
    ffn_share = lax.psum_scatter(
        jnp.concatenate([term_in, term_down], axis=1).astype(jnp.bfloat16),
        "seq",
        scatter_dimension=0,
        tiled=True,
    ).astype(jnp.float32)
    share_in = ffn_share[:, :model_width]
    share_down = ffn_share[:, model_width:]
    grad_qkv_flat = grad_qkv.reshape(token_count, 3 * model_width)
    term_qkv = jnp.einsum("tr,te->re", resid_low, grad_qkv_flat, preferred_element_type=jnp.float32)
    term_out = jnp.einsum("tr,te->re", mixed_rows, grad_attn, preferred_element_type=jnp.float32)
    term_time = jnp.einsum("tr,te->re", time_embed, grad_time, preferred_element_type=jnp.float32)
    attn_share = lax.psum_scatter(
        jnp.concatenate([term_qkv, term_out, term_time], axis=1).astype(jnp.bfloat16),
        "seq",
        scatter_dimension=0,
        tiled=True,
    ).astype(jnp.float32)
    sum_in, sum_down, sum_attn = lax.psum((share_in, share_down, attn_share), "dp")
    (
        grad_b_query,
        grad_b_value,
        grad_b_out,
        grad_b_time,
        grad_b_in,
        grad_b_down,
        sum_gain_one,
        sum_shift_one,
        sum_gain_two,
        sum_shift_two,
    ) = lax.psum(
        (
            jnp.sum(grad_query_rows, axis=0, dtype=jnp.float32),
            jnp.sum(grad_value_rows, axis=0, dtype=jnp.float32),
            jnp.sum(grad_attn, axis=0, dtype=jnp.float32),
            jnp.sum(grad_time, axis=0, dtype=jnp.float32),
            jnp.sum(grad_pre, axis=0, dtype=jnp.float32),
            jnp.sum(grad_ffn, axis=0, dtype=jnp.float32),
            grad_gain_one,
            grad_shift_one,
            grad_gain_two,
            grad_shift_two,
        ),
        ("dp", "seq"),
    )
    return (
        layer_out,
        grad_tokens,
        sum_attn[:, :model_width],
        sum_attn[:, model_width : 2 * model_width],
        sum_attn[:, 2 * model_width : 3 * model_width],
        sum_attn[:, 3 * model_width : 4 * model_width],
        sum_attn[:, 4 * model_width :],
        sum_in,
        sum_down,
        grad_b_query,
        grad_b_value,
        grad_b_out,
        grad_b_time,
        grad_b_in,
        grad_b_down,
        sum_gain_one,
        sum_shift_one,
        sum_gain_two,
        sum_shift_two,
    )


def solution(mesh):
    in_specs = (
        P(("dp", "seq"), None),
        P(("dp", "seq"), None),
        P("dp"),
        P(("dp", "seq"), None),
        P("seq", None),
        P("seq", None),
        P("seq", None),
        P("seq", None),
        P("seq", None),
        P("seq", None),
        P("seq", None),
        P(),
        P(),
        P(),
        P(),
        P(),
        P(),
        P(),
        P(),
        P(),
        P(),
    )
    out_specs = (
        P(("dp", "seq"), None),
        P(("dp", "seq"), None),
        P("seq", None),
        P("seq", None),
        P("seq", None),
        P("seq", None),
        P("seq", None),
        P("seq", None),
        P("seq", None),
        P(),
        P(),
        P(),
        P(),
        P(),
        P(),
        P(),
        P(),
        P(),
        P(),
    )
    return jax.shard_map(local, mesh=mesh, in_specs=in_specs, out_specs=out_specs, check_vma=False)
```

profile of v0, /device:TPU:0, one launch (start us, length us, event | category | flops | bytes accessed | tf_op | source)
XLA Modules:
  0.0 1024.9 jit_solution(11175937221474394372)
XLA Ops:
  11.2 23.7 %all-gather.8.cloned.1.call-done = bf16[1024,1024]{1,0:T(8,128)(2,1)} async-done(((bf16[256,1024]{1,0:T(8,128)(2,1)}), bf16[1024,1024]{1,0:T(8,128)(2,1)}) %all-gather.8.cloned.1.call-update) | async-done | bytes 2097168 | tf_op jit(solution)/shard_map/all_gather | solution.py:122
  36.9 22.2 %all-gather.12.cloned.1.call-done = bf16[1024,1024]{1,0:T(8,128)(2,1)} async-done(((bf16[256,1024]{1,0:T(8,128)(2,1)}), bf16[1024,1024]{1,0:T(8,128)(2,1)}) %all-gather.12.cloned.1.call-update) | async-done | bytes 2097168 | tf_op jit(solution)/shard_map/all_gather | solution.py:119
  62.9 20.3 %all-gather.10.cloned.1.call-done = bf16[1024,1024]{1,0:T(8,128)(2,1)} async-done(((bf16[256,1024]{1,0:T(8,128)(2,1)}), bf16[1024,1024]{1,0:T(8,128)(2,1)}) %all-gather.10.cloned.1.call-update) | async-done | bytes 2097168 | tf_op jit(solution)/shard_map/all_gather | solution.py:118
  87.1 20.2 %all-gather.14.cloned.1.call-done = bf16[1024,1024]{1,0:T(8,128)(2,1)} async-done(((bf16[256,1024]{1,0:T(8,128)(2,1)}), bf16[1024,1024]{1,0:T(8,128)(2,1)}) %all-gather.14.cloned.1.call-update) | async-done | bytes 2097168 | tf_op jit(solution)/shard_map/all_gather | solution.py:120
  122.3 77.5 %all-to-all-done = bf16[1,512,3,1024]{1,2,0,3:T(4,128)(2,1)} async-done(((bf16[1,512,3,1024]{1,2,0,3:T(4,128)(2,1)}), bf16[1,512,3,1024]{1,2,0,3:T(4,128)(2,1)}, u32[]{:S(2)}, u32[]{:S(2)}) %all-to-all-start) | async-done | bytes 3145760 | tf_op jit(solution)/shard_map/all_to_all | solution.py:155
  202.9 16.3 %while.22 = (s32[]{:T(128)}, bf16[4,512,256]{1,2,0:T(8,128)(2,1)}, f32[4,4,512]{2,1,0:T(4,128)S(1)}, bf16[4,512,3,256]{1,3,2,0:T(8,128)(2,1)S(1)}, pred[4,512]{1,0:T(4,128)(4,1)S(1)}, /*index=5*/s32[]{:T(128)}) while((s32[]{:T(128)}, bf16[4,512,256]{1,2,0:T(8,128)(2,1)}, f32[4,4,512]{2,1,0:T(4,128)S(1)}, ...), condition=%wide.region_3.4_spmd, body=%wide.region_0.3_spmd.sunk | while | flops 281147392 | bytes 17370192 | solution.py:156
  223.7 18.0 %all-to-all-done.1 = bf16[4,512,256]{1,2,0:T(8,128)(2,1)} async-done(((bf16[4,512,256]{1,2,0:T(8,128)(2,1)}), bf16[4,512,256]{1,2,0:T(8,128)(2,1)}, u32[]{:S(2)}, u32[]{:S(2)}) %all-to-all-start.1) | async-done | bytes 1048608 | tf_op jit(solution)/shard_map/all_to_all | solution.py:157
  247.0 27.2 %multiply_convert_fusion.1 = (bf16[512,4096]{1,0:T(8,128)(2,1)}, f32[512,4096]{1,0:T(8,128)}, f32[512,4096]{1,0:T(8,128)}) fusion(f32[4096]{0:T(1024)S(1)} %convert_element_type.170, bf16[4096,1024]{1,0:T(8,128)(2,1)} %all-gather.18.cloned.1.call-done, f32[512,1024]{1,0:T(8,128)} %copy-done, f32[1024]{0:T(1024)S(1)} %convert_element_type.168, ...), kind=kOutput, calls=%fused_computation.37 | convolution fusion | flops 4436000768 | bytes 31485952 | tf_op jit(solution)/shard_map/td,fd->tf/dot_general | solution.py:164
  274.2 10.3 %all-gather.20.cloned.1.call-done = bf16[4096,1024]{1,0:T(8,128)(2,1)} async-done(((bf16[1024,1024]{1,0:T(8,128)(2,1)}), bf16[4096,1024]{1,0:T(8,128)(2,1)}) %all-gather.20.cloned.1.call-update) | async-done | bytes 8388624 | tf_op jit(solution)/shard_map/all_gather | solution.py:124
  284.5 10.0 fusion.59
  300.6 7.1 convolution_convert_fusion
  307.7 13.5 %convert_reduce_fusion = (f32[4096]{0:T(1024)S(1)}, bf16[512,4096]{1,0:T(8,128)(2,1)S(1)}) fusion(f32[512,4096]{1,0:T(8,128)} %get-tuple-element.209, f32[512,4096]{1,0:T(8,128)} %get-tuple-element.234, f32[4096]{0:T(1024)S(1)} %convert_element_type.170, bf16[512,1024]{1,0:T(8,128)(2,1)S(1)} %get-tuple-element.199, ...), kind=kOutput, calls=%fused_computation.35 | convolution fusion | flops 4330614784 | bytes 30441472 | tf_op jit(solution)/shard_map/td,fd->tf/dot_general | solution.py:183
  321.3 7.0 convolution_convert_fusion.1
  328.3 13.9 %pad_maximum_fusion = bf16[4096,2048]{0,1:T(8,128)(2,1)} fusion(bf16[4096,1024]{0,1:T(8,128)(2,1)} %convolution_convert_fusion, bf16[4096,1024]{0,1:T(8,128)(2,1)} %convolution_convert_fusion.1), kind=kLoop, calls=%fused_computation.31 | loop fusion | flops 33554432 | bytes 33554432 | tf_op jit(solution)/shard_map/concatenate | solution.py:221
  342.2 11.4 %multiply_reduce_fusion.2 = (f32[1024]{0:T(1024)S(1)}, f32[512]{0:T(512)S(1)}, f32[1024]{0:T(1024)S(1)}, f32[512,1024]{1,0:T(8,128)S(1)}) fusion(f32[512,1024]{1,0:T(8,128)} %copy-done, f32[512]{0:T(512)S(1)} %fusion.42, f32[512]{0:T(512)S(1)} %broadcast_multiply_fusion.1, f32[1024]{0:T(1024)S(1)} %convert_element_type.167, ...), kind=kOutput, calls=%fused_computation.61 | convolution fusion | flops 4300207616 | bytes 18894848 | tf_op jit(solution)/shard_map/dot_general | solution.py:185
  365.9 9.0 reduce.7
  383.1 26.1 %all-to-all-done.2 = bf16[4,2,65536]{2,1,0:T(2,128)(2,1)} async-done(((bf16[4,2,65536]{2,1,0:T(2,128)(2,1)}), bf16[4,2,65536]{2,1,0:T(2,128)(2,1)}, u32[]{:S(2)}, u32[]{:S(2)}) %all-to-all-start.2) | async-done | bytes 1048608 | tf_op jit(solution)/shard_map/all_to_all | solution.py:191
  416.1 35.0 %while.23 = (s32[]{:T(128)}, bf16[4,512,3,256]{1,3,2,0:T(8,128)(2,1)}, bf16[4,512,3,256]{1,3,2,0:T(8,128)(2,1)S(1)}, pred[4,512]{1,0:T(4,128)(4,1)S(1)}, f32[4,4...) while((s32[]{:T(128)}, bf16[4,512,3,256]{1,3,2,0:T(8,128)(2,1)}, ...), condition=%wide.region_14.15_spmd, body=%wide.region_12.14_spmd.sunk | while | flops 689829888 | bytes 39382108 | solution.py:198
  459.2 51.5 %all-to-all-done.3 = bf16[4,512,3,256]{1,3,2,0:T(8,128)(2,1)S(1)} async-done(((bf16[4,512,3,256]{1,3,2,0:T(8,128)(2,1)}), bf16[4,512,3,256]{1,3,2,0:T(8,128)(2,1)S(1)}, u32[]{:S(2)}, u32[]{:S(2)}) %all-to-all-start.3) | async-done | bytes 3145760 | tf_op jit(solution)/shard_map/all_to_all | solution.py:199
  524.0 9.9 pad_maximum_fusion.1
  548.6 41.3 %all-reduce = (f32[1024]{0:T(1024)}, f32[1024]{0:T(1024)}, f32[1024]{0:T(1024)}, f32[1024]{0:T(1024)}, f32[4096]{0:T(1024)}, /*index=5*/f32[1024]{0:T(1024)}, f3...) all-reduce(f32[1024]{0:T(1024)S(1)} %get-tuple-element.240, ...), channel_id=1, replica_groups=mesh['dp'=8,'seq'=4] {'dp','seq'}, use_global_device_ids=true, to_apply=%region_22.23 | all-reduce | flops 13312 | bytes 104448 | tf_op jit(solution)/shard_map/psum | solution.py:250
  589.9 29.4 %reduce-scatter.3.cloned.1.call-done = bf16[256,5120]{1,0:T(8,128)(2,1)} async-done(((bf16[1024,5120]{1,0:T(8,128)(2,1)}), bf16[256,5120]{1,0:T(8,128)(2,1)}) %reduce-scatter.3.cloned.1.call-update) | async-done | bytes 2621456 | tf_op jit(solution)/shard_map/reduce_scatter | solution.py:232
  619.3 267.7 %all-reduce.6 = f32[256,5120]{1,0:T(8,128)} all-reduce(bf16[256,5120]{1,0:T(8,128)(2,1)} %reduce-scatter.3.cloned.1.call-done), channel_id=1, replica_groups=mesh['dp'=8,'seq'=4] {'dp'}, use_global_device_ids=true, to_apply=%region_17.18 | all-reduce | flops 1310720 | bytes 7864320 | tf_op jit(solution)/shard_map/psum | solution.py:238
  892.0 114.9 %all-reduce.5.cloned.1.call-done = (f32[1024,1024]{0,1:T(8,128)}, f32[1024,1024]{0,1:T(8,128)}) async-done(((f32[1024,1024]{0,1:T(8,128)}, f32[1024,1024]{0,1:T(8,128)}), (f32[1024,1024]{0,1:T(8,128)}, f32[1024,1024]{0,1:T(8,128)})) %all-reduce.5.cloned.1.call-update) | async-done | bytes 8388624 | tf_op jit(solution)/shard_map/psum | solution.py:238
  (250 shorter events, 177.1 us)
Async XLA Ops:
  7.2 27.7 %copy-start.22 = (bf16[1,1024]{1,0:T(2,128)(2,1)S(1)}, bf16[1,1024]{1,0:T(2,128)(2,1)}, u32[]{:S(2)}) copy-start(bf16[1,1024]{1,0:T(2,128)(2,1)} %param.26) | copy-start | bytes 6148
  7.2 29.7 %copy-start.27 = (bf16[1024]{0:T(1024)(128)(2,1)S(1)}, bf16[1024]{0:T(1024)(128)(2,1)}, u32[]{:S(2)}) copy-start(bf16[1024]{0:T(1024)(128)(2,1)} %param.39) | copy-start | bytes 6148
  7.2 51.9 %copy-start.12 = (bf16[512,1024]{1,0:T(8,128)(2,1)S(1)}, bf16[512,1024]{1,0:T(8,128)(2,1)}, u32[]{:S(2)}) copy-start(bf16[512,1024]{1,0:T(8,128)(2,1)} %param.25) | copy-start | bytes 3145732
  7.2 27.7 %all-gather.8.cloned.1.call-start = ((), (), s32[]{:S(2)}) async-start(), calls=%async_computation.6 | async-start | bytes 2621440 | tf_op jit(solution)/shard_map/all_gather | solution.py:122
  8.0 51.1 %all-gather.12.cloned.1.call-start = ((), (), s32[]{:S(2)}) async-start(), calls=%async_computation.8 | async-start | bytes 2621440 | tf_op jit(solution)/shard_map/all_gather | solution.py:119
  8.7 74.5 %all-gather.10.cloned.1.call-start = ((), (), s32[]{:S(2)}) async-start(), calls=%async_computation.7 | async-start | bytes 2621440 | tf_op jit(solution)/shard_map/all_gather | solution.py:118
  9.5 97.8 %all-gather.14.cloned.1.call-start = ((), (), s32[]{:S(2)}) async-start(), calls=%async_computation.9 | async-start | bytes 2621440 | tf_op jit(solution)/shard_map/all_gather | solution.py:120
  10.0 213.6 %all-gather.16.cloned.1.call-start = ((), (), s32[]{:S(2)}) async-start(), calls=%async_computation.10 | async-start | bytes 2621440 | tf_op jit(solution)/shard_map/all_gather | solution.py:121
  10.6 236.4 %all-gather.18.cloned.1.call-start = ((), (), s32[]{:S(2)}) async-start(), calls=%async_computation.11 | async-start | bytes 10485760 | tf_op jit(solution)/shard_map/all_gather | solution.py:123
  36.9 204.8 %copy-start.16 = (f32[1024]{0:T(1024)}, f32[1024]{0:T(1024)S(1)}, u32[]{:S(2)}) copy-start(f32[1024]{0:T(1024)S(1)} %convert_add_fusion.1) | copy-start | bytes 12292
  116.3 83.5 %all-to-all-start = ((bf16[1,512,3,1024]{1,2,0,3:T(4,128)(2,1)}), bf16[1,512,3,1024]{1,2,0,3:T(4,128)(2,1)}, u32[]{:S(2)}, u32[]{:S(2)}) async-start(bf16[1,512,3,1024]{1,2,0,3:T(4,128)(2,1)} %copy.80), calls=%async_computation | async-start | bytes 8388608 | tf_op jit(solution)/shard_map/all_to_all | solution.py:155
  121.4 163.1 %all-gather.20.cloned.1.call-start = ((), (), s32[]{:S(2)}) async-start(), calls=%async_computation.12 | async-start | bytes 10485760 | tf_op jit(solution)/shard_map/all_gather | solution.py:124
  202.8 20.7 %copy-start.29 = (bf16[1024]{0:T(1024)(128)(2,1)S(1)}, bf16[1024]{0:T(1024)(128)(2,1)}, u32[]{:S(2)}) copy-start(bf16[1024]{0:T(1024)(128)(2,1)} %param.42) | copy-start | bytes 6148
  202.8 20.7 %copy-start.30 = (bf16[1024]{0:T(1024)(128)(2,1)S(1)}, bf16[1024]{0:T(1024)(128)(2,1)}, u32[]{:S(2)}) copy-start(bf16[1024]{0:T(1024)(128)(2,1)} %param.43) | copy-start | bytes 6148
  202.8 20.7 %copy-start.24 = (bf16[4096]{0:T(1024)(128)(2,1)S(1)}, bf16[4096]{0:T(1024)(128)(2,1)}, u32[]{:S(2)}) copy-start(bf16[4096]{0:T(1024)(128)(2,1)} %param.40) | copy-start | bytes 24580
  202.8 20.7 %copy-start.31 = (bf16[1024]{0:T(1024)(128)(2,1)S(1)}, bf16[1024]{0:T(1024)(128)(2,1)}, u32[]{:S(2)}) copy-start(bf16[1024]{0:T(1024)(128)(2,1)} %param.41) | copy-start | bytes 6148
  202.9 20.7 %copy-start.32 = (bf16[1024]{0:T(1024)(128)(2,1)S(1)}, bf16[1024]{0:T(1024)(128)(2,1)}, u32[]{:S(2)}) copy-start(bf16[1024]{0:T(1024)(128)(2,1)} %param.44) | copy-start | bytes 6148
  202.9 20.7 %copy-start.33 = (bf16[1024]{0:T(1024)(128)(2,1)S(1)}, bf16[1024]{0:T(1024)(128)(2,1)}, u32[]{:S(2)}) copy-start(bf16[1024]{0:T(1024)(128)(2,1)} %param.45) | copy-start | bytes 6148
  219.2 22.5 %all-to-all-start.1 = ((bf16[4,512,256]{1,2,0:T(8,128)(2,1)}), bf16[4,512,256]{1,2,0:T(8,128)(2,1)}, u32[]{:S(2)}, u32[]{:S(2)}) async-start(bf16[4,512,256]{1,2,0:T(8,128)(2,1)} %get-tuple-element.79), calls=%async_computation.1 | async-start | bytes 2097152 | tf_op jit(solution)/shard_map/all_to_all | solution.py:157
  223.4 310.5 %reduce-scatter.5.cloned.1.call-start = ((), (), s32[]{:S(2)}) async-start(), calls=%async_computation.14 | async-start | bytes 20971520 | tf_op jit(solution)/shard_map/reduce_scatter | solution.py:220
  378.8 30.4 %all-to-all-start.2 = ((bf16[4,2,65536]{2,1,0:T(2,128)(2,1)}), bf16[4,2,65536]{2,1,0:T(2,128)(2,1)}, u32[]{:S(2)}, u32[]{:S(2)}) async-start(bf16[4,2,65536]{2,1,0:T(2,128)(2,1)} %reshape.269), calls=%async_computation.2 | async-start | bytes 2097152 | tf_op jit(solution)/shard_map/all_to_all | solution.py:191
  451.1 59.6 %all-to-all-start.3 = ((bf16[4,512,3,256]{1,3,2,0:T(8,128)(2,1)}), bf16[4,512,3,256]{1,3,2,0:T(8,128)(2,1)S(1)}, u32[]{:S(2)}, u32[]{:S(2)}) async-start(bf16[4,512,3,256]{1,3,2,0:T(8,128)(2,1)} %get-tuple-element.81), calls=%async_computation.3 | async-start | bytes 6291456 | tf_op jit(solution)/shard_map/all_to_all | solution.py:199
  454.9 164.4 %reduce-scatter.3.cloned.1.call-start = ((), (), s32[]{:S(2)}) async-start(), calls=%async_computation.13 | async-start | bytes 13107200 | tf_op jit(solution)/shard_map/reduce_scatter | solution.py:232
  533.9 473.0 %all-reduce.5.cloned.1.call-start = ((), (), s32[]{:S(2)}) async-start(), calls=%async_computation.15 | async-start | bytes 16777216 | tf_op jit(solution)/shard_map/psum | solution.py:238
  (30 other events, 144.6 us)
Sparse Core Ops, SparseCore 0:
  9.6 25.2 all-gather.7
  36.5 22.5 all-gather.11
  60.7 22.5 all-gather.9
  84.7 22.5 all-gather.13
  108.7 27.7 all-gather.15
  137.9 83.4 all-gather.17
  223.0 61.5 all-gather.19
  342.3 155.0 reduce-scatter.4
  534.0 85.2 reduce-scatter.2
  624.4 382.4 all-reduce.4
where the time goes:
time: 1030 us; the launch traced here: 1020 us
  waiting for transfers between devices  419 us (41%)
  blocking collectives  309 us (30%)
  matrix products  135 us (13%)
  local copies, waits for them, and re-layouts  75.6 us (7%)
  other arithmetic  52.9 us (5%)
  starting transfers between devices  17.8 us (2%)
  between operations  15.3 us (1%)
    psum x1, blocking collectives, local(): lax.psum((share_in, share_down, attn_share), 'dp')  268 us
    psum x1, waiting for transfers between devices, local(): lax.psum((share_in, share_down, attn_share), 'dp')  115 us
    all_to_all x1, waiting for transfers between devices, local(): lax.all_to_all(stacked, 'seq', split_axis=3, concat_axis=0, tiled=True)  77.5 us
    all_to_all x1, waiting for transfers between devices, local(): lax.all_to_all(grad_stack, 'seq', split_axis=0, concat_axis=3, tiled=True)  51.5 us
    psum x1, blocking collectives, local(): lax.psum((jnp.sum(grad_query_rows, axis=0, dtype=jnp.float32), jnp.sum(gr...  41.3 us
    unnamed x86, local copies, waits for them, and re-layouts  32.8 us
    reduce_scatter x1, waiting for transfers between devices, local(): lax.psum_scatter(jnp.concatenate([term_qkv, term_out, term_time], axis=1)...  29.4 us
    dot_general x1, matrix products, local(): jnp.einsum('td,fd->tf', first_low, full_in, preferred_element_type=jnp.fl...  27.2 us
  transfers between devices with their start and end apart: 14, of which 11 were waited for; matrix products, arithmetic and copies ran while one was open for 18% of the time, Pallas kernels for 0%

commit v1 on v0

--- a/solution.py
+++ b/solution.py
@@ -152,7 +152,19 @@
     stacked = jnp.stack([query_rows, key_rows, value_rows], axis=1).reshape(
         item_count, slot_count, 3, model_width
     )
-    head_side = lax.all_to_all(stacked, "seq", split_axis=3, concat_axis=0, tiled=True)
+    ways, here = (lax.axis_size("seq"), lax.axis_index("seq"))
+    width = stacked.shape[3] // ways
+    shape = list(stacked.shape)
+    shape[3] = width
+    height = shape[0]
+    shape[0] = height * ways
+    full = jnp.zeros(shape, stacked.dtype)
+    for mask in range(ways):
+        part = lax.dynamic_slice_in_dim(stacked, (here ^ mask) * width, width, axis=3)
+        if mask:
+            part = lax.ppermute(part, "seq", [(d, d ^ mask) for d in range(ways)])
+        full = lax.dynamic_update_slice_in_dim(full, part, (here ^ mask) * height, axis=0)
+    head_side = full
     mixed_heads, log_totals = lax.map(attend_forward, (head_side, group_valid))
     mixed_rows = lax.all_to_all(
         mixed_heads, "seq", split_axis=0, concat_axis=2, tiled=True

time: 1030 us -> 1030 us (level)
  waiting for transfers between devices: 419 us -> 385 us
  blocking collectives: 309 us -> 337 us
    all_to_all x2 -> x0, waiting for transfers between devices: 104 us -> none  [the longest x1 77.5 us: local(): lax.all_to_all(stacked, 'seq', split_axis=3, concat_axis=0, tiled=True)]
    ppermute x0 -> x3, waiting for transfers between devices: none -> 40.1 us  [local(): part = lax.ppermute(part, 'seq', [(d, d ^ mask) for d in range(ways)])]
    all_to_all x0 -> x1, blocking collectives: none -> 30.4 us  [local(): lax.all_to_all(grad_mixed.reshape(item_count, slot_count, model_width), '...]
    all_gather x1, waiting for transfers between devices: 10.3 us -> 31.6 us  [local(): lax.all_gather(w_down, 'seq', axis=0, tiled=True)]
    unnamed x86 -> x84, local copies, waits for them, and re-layouts: 32.8 us -> 34.3 us
  transfers between devices with their start and end apart: 14 -> 15, of which waited for: 11 -> 11; matrix products, arithmetic and copies ran while one was open for 18% -> 19% of each run, Pallas kernels for 0% -> 0%
where the time goes in v1:
time: 1030 us; the launch traced here: 1020 us
  waiting for transfers between devices  385 us (37%)
  blocking collectives  337 us (33%)
  matrix products  133 us (13%)
  local copies, waits for them, and re-layouts  83.8 us (8%)
  other arithmetic  52.9 us (5%)
  between operations  15.4 us (1%)
  starting transfers between devices  10.5 us (1%)
    psum x1, blocking collectives, local(): lax.psum((share_in, share_down, attn_share), 'dp')  265 us
    psum x1, waiting for transfers between devices, local(): lax.psum((share_in, share_down, attn_share), 'dp')  117 us
    all_to_all x1, waiting for transfers between devices, local(): lax.all_to_all(grad_stack, 'seq', split_axis=0, concat_axis=3, tiled=True)  49 us
    psum x1, blocking collectives, local(): lax.psum((jnp.sum(grad_query_rows, axis=0, dtype=jnp.float32), jnp.sum(gr...  41.6 us
    ppermute x3, waiting for transfers between devices, local(): part = lax.ppermute(part, 'seq', [(d, d ^ mask) for d in range(ways)])  40.1 us
    unnamed x84, local copies, waits for them, and re-layouts  34.3 us
    all_gather x1, waiting for transfers between devices, local(): lax.all_gather(w_down, 'seq', axis=0, tiled=True)  31.6 us
    all_to_all x1, blocking collectives, local(): lax.all_to_all(grad_mixed.reshape(item_count, slot_count, model_width), '...  30.4 us
  transfers between devices with their start and end apart: 15, of which 11 were waited for; matrix products, arithmetic and copies ran while one was open for 19% of the time, Pallas kernels for 0%

profile of v1, /device:TPU:0, one launch (start us, length us, event | category | flops | bytes accessed | tf_op | source)
XLA Modules:
  0.0 1017.8 jit_solution(15716176928645232391)
XLA Ops:
  11.3 23.6 %all-gather.8.cloned.1.call-done = bf16[1024,1024]{1,0:T(8,128)(2,1)} async-done(((bf16[256,1024]{1,0:T(8,128)(2,1)}), bf16[1024,1024]{1,0:T(8,128)(2,1)}) %all-gather.8.cloned.1.call-update) | async-done | bytes 2097168 | tf_op jit(solution)/shard_map/all_gather | solution.py:122
  36.9 22.2 %all-gather.12.cloned.1.call-done = bf16[1024,1024]{1,0:T(8,128)(2,1)} async-done(((bf16[256,1024]{1,0:T(8,128)(2,1)}), bf16[1024,1024]{1,0:T(8,128)(2,1)}) %all-gather.12.cloned.1.call-update) | async-done | bytes 2097168 | tf_op jit(solution)/shard_map/all_gather | solution.py:119
  61.9 21.3 %all-gather.10.cloned.1.call-done = bf16[1024,1024]{1,0:T(8,128)(2,1)} async-done(((bf16[256,1024]{1,0:T(8,128)(2,1)}), bf16[1024,1024]{1,0:T(8,128)(2,1)}) %all-gather.10.cloned.1.call-update) | async-done | bytes 2097168 | tf_op jit(solution)/shard_map/all_gather | solution.py:118
  86.1 21.2 %all-gather.14.cloned.1.call-done = bf16[1024,1024]{1,0:T(8,128)(2,1)} async-done(((bf16[256,1024]{1,0:T(8,128)(2,1)}), bf16[1024,1024]{1,0:T(8,128)(2,1)}) %all-gather.14.cloned.1.call-update) | async-done | bytes 2097168 | tf_op jit(solution)/shard_map/all_gather | solution.py:120
  118.8 25.4 %collective-permute-done.1 = bf16[1,512,3,256]{3,1,2,0:T(8,128)(2,1)} collective-permute-done((bf16[1,512,3,256]{3,1,2,0:T(8,128)(2,1)}, bf16[1,512,3,256]{3,1,2,0:T(8,128)(2,1)}, u32[]{:S(2)}, u32[]{:S(2)}) %collective-permute-start.1) | collective-permute-done | bytes 786464 | tf_op jit(solution)/shard_map/ppermute | solution.py:165
  148.9 14.7 %collective-permute-done.2 = bf16[1,512,3,256]{3,1,2,0:T(8,128)(2,1)} collective-permute-done((bf16[1,512,3,256]{3,1,2,0:T(8,128)(2,1)}, bf16[1,512,3,256]{3,1,2,0:T(8,128)(2,1)}, u32[]{:S(2)}, u32[]{:S(2)}) %collective-permute-start.2) | collective-permute-done | bytes 786464 | tf_op jit(solution)/shard_map/ppermute | solution.py:165
  167.2 16.3 %while.22 = (s32[]{:T(128)}, bf16[4,512,256]{1,2,0:T(8,128)(2,1)}, f32[4,4,512]{2,1,0:T(4,128)S(1)}, bf16[4,512,3,256]{1,3,2,0:T(8,128)(2,1)S(1)}, pred[4,512]{1,0:T(4,128)(4,1)S(1)}, /*index=5*/s32[]{:T(128)}) while((s32[]{:T(128)}, bf16[4,512,256]{1,2,0:T(8,128)(2,1)}, f32[4,4,512]{2,1,0:T(4,128)S(1)}, ...), condition=%wide.region_3.4_spmd, body=%wide.region_0.3_spmd.sunk | while | flops 281147392 | bytes 17370192 | solution.py:168
  188.0 26.0 %all-to-all-done = bf16[4,512,256]{1,2,0:T(8,128)(2,1)} async-done(((bf16[4,512,256]{1,2,0:T(8,128)(2,1)}), bf16[4,512,256]{1,2,0:T(8,128)(2,1)}, u32[]{:S(2)}, u32[]{:S(2)}) %all-to-all-start) | async-done | bytes 1048608 | tf_op jit(solution)/shard_map/all_to_all | solution.py:169
  219.3 27.2 %multiply_convert_fusion.1 = (bf16[512,4096]{1,0:T(8,128)(2,1)}, f32[512,4096]{1,0:T(8,128)}, f32[512,4096]{1,0:T(8,128)}) fusion(f32[4096]{0:T(1024)S(1)} %convert_element_type.170, bf16[4096,1024]{1,0:T(8,128)(2,1)} %all-gather.18.cloned.1.call-done, f32[512,1024]{1,0:T(8,128)} %copy-done, f32[1024]{0:T(1024)S(1)} %convert_element_type.168, ...), kind=kOutput, calls=%fused_computation.37 | convolution fusion | flops 4436000768 | bytes 31485952 | tf_op jit(solution)/shard_map/td,fd->tf/dot_general | solution.py:176
  246.5 31.6 %all-gather.20.cloned.1.call-done = bf16[4096,1024]{1,0:T(8,128)(2,1)} async-done(((bf16[1024,1024]{1,0:T(8,128)(2,1)}), bf16[4096,1024]{1,0:T(8,128)(2,1)}) %all-gather.20.cloned.1.call-update) | async-done | bytes 8388624 | tf_op jit(solution)/shard_map/all_gather | solution.py:124
  278.1 10.0 fusion.59
  294.1 7.1 convolution_convert_fusion
  301.3 13.5 %convert_reduce_fusion = (f32[4096]{0:T(1024)S(1)}, bf16[512,4096]{1,0:T(8,128)(2,1)S(1)}) fusion(f32[512,4096]{1,0:T(8,128)} %get-tuple-element.209, f32[512,4096]{1,0:T(8,128)} %get-tuple-element.238, f32[4096]{0:T(1024)S(1)} %convert_element_type.170, bf16[512,1024]{1,0:T(8,128)(2,1)S(1)} %get-tuple-element.199, ...), kind=kOutput, calls=%fused_computation.35 | convolution fusion | flops 4330614784 | bytes 30441472 | tf_op jit(solution)/shard_map/td,fd->tf/dot_general | solution.py:195
  321.8 13.8 %pad_maximum_fusion = bf16[4096,2048]{0,1:T(8,128)(2,1)} fusion(bf16[4096,1024]{0,1:T(8,128)(2,1)} %convolution_convert_fusion, bf16[4096,1024]{0,1:T(8,128)(2,1)} %convolution_convert_fusion.1), kind=kLoop, calls=%fused_computation.31 | loop fusion | flops 33554432 | bytes 33554432 | tf_op jit(solution)/shard_map/concatenate | solution.py:233
  335.7 11.4 %multiply_reduce_fusion.2 = (f32[1024]{0:T(1024)S(1)}, f32[512]{0:T(512)S(1)}, f32[1024]{0:T(1024)S(1)}, f32[512,1024]{1,0:T(8,128)S(1)}) fusion(f32[512,1024]{1,0:T(8,128)} %copy-done, f32[512]{0:T(512)S(1)} %fusion.42, f32[512]{0:T(512)S(1)} %broadcast_multiply_fusion.1, f32[1024]{0:T(1024)S(1)} %convert_element_type.167, ...), kind=kOutput, calls=%fused_computation.60 | convolution fusion | flops 4300207616 | bytes 18894848 | tf_op jit(solution)/shard_map/dot_general | solution.py:197
  359.9 9.0 reduce.7
  372.9 30.4 %all_to_all.48 = bf16[4,2,65536]{2,1,0:T(2,128)(2,1)} all-to-all(bf16[4,2,65536]{2,1,0:T(2,128)(2,1)} %reshape.270), channel_id=1, replica_groups=mesh['dp'=8,'seq'=4] {'seq'}, dimensions={0} | all-to-all | bytes 2097152 | tf_op jit(solution)/shard_map/all_to_all | solution.py:203
  412.0 35.0 %while.23 = (s32[]{:T(128)}, bf16[4,512,3,256]{1,3,2,0:T(8,128)(2,1)}, bf16[4,512,3,256]{1,3,2,0:T(8,128)(2,1)S(1)}, pred[4,512]{1,0:T(4,128)(4,1)S(1)}, f32[4,4...) while((s32[]{:T(128)}, bf16[4,512,3,256]{1,3,2,0:T(8,128)(2,1)}, ...), condition=%wide.region_14.15_spmd, body=%wide.region_12.14_spmd.sunk | while | flops 689829888 | bytes 39382108 | solution.py:210
  455.2 49.0 %all-to-all-done.2 = bf16[4,512,3,256]{1,3,2,0:T(8,128)(2,1)S(1)} async-done(((bf16[4,512,3,256]{1,3,2,0:T(8,128)(2,1)}), bf16[4,512,3,256]{1,3,2,0:T(8,128)(2,1)S(1)}, u32[]{:S(2)}, u32[]{:S(2)}) %all-to-all-start.2) | async-done | bytes 3145760 | tf_op jit(solution)/shard_map/all_to_all | solution.py:211
  517.2 9.9 pad_maximum_fusion.1
  541.8 41.6 %all-reduce = (f32[1024]{0:T(1024)}, f32[1024]{0:T(1024)}, f32[1024]{0:T(1024)}, f32[1024]{0:T(1024)}, f32[4096]{0:T(1024)}, /*index=5*/f32[1024]{0:T(1024)}, f3...) all-reduce(f32[1024]{0:T(1024)S(1)} %get-tuple-element.244, ...), channel_id=1, replica_groups=mesh['dp'=8,'seq'=4] {'dp','seq'}, use_global_device_ids=true, to_apply=%region_22.23 | all-reduce | flops 13312 | bytes 104448 | tf_op jit(solution)/shard_map/psum | solution.py:262
  583.4 29.1 %reduce-scatter.3.cloned.1.call-done = bf16[256,5120]{1,0:T(8,128)(2,1)} async-done(((bf16[1024,5120]{1,0:T(8,128)(2,1)}), bf16[256,5120]{1,0:T(8,128)(2,1)}) %reduce-scatter.3.cloned.1.call-update) | async-done | bytes 2621456 | tf_op jit(solution)/shard_map/reduce_scatter | solution.py:244
  612.5 264.9 %all-reduce.6 = f32[256,5120]{1,0:T(8,128)} all-reduce(bf16[256,5120]{1,0:T(8,128)(2,1)} %reduce-scatter.3.cloned.1.call-done), channel_id=1, replica_groups=mesh['dp'=8,'seq'=4] {'dp'}, use_global_device_ids=true, to_apply=%region_17.18 | all-reduce | flops 1310720 | bytes 7864320 | tf_op jit(solution)/shard_map/psum | solution.py:250
  882.4 117.5 %all-reduce.5.cloned.1.call-done = (f32[1024,1024]{0,1:T(8,128)}, f32[1024,1024]{0,1:T(8,128)}) async-done(((f32[1024,1024]{0,1:T(8,128)}, f32[1024,1024]{0,1:T(8,128)}), (f32[1024,1024]{0,1:T(8,128)}, f32[1024,1024]{0,1:T(8,128)})) %all-reduce.5.cloned.1.call-update) | async-done | bytes 8388624 | tf_op jit(solution)/shard_map/psum | solution.py:250
  (259 shorter events, 181.9 us)
Async XLA Ops:
  7.2 27.7 %copy-start.21 = (bf16[1,1024]{1,0:T(2,128)(2,1)S(1)}, bf16[1,1024]{1,0:T(2,128)(2,1)}, u32[]{:S(2)}) copy-start(bf16[1,1024]{1,0:T(2,128)(2,1)} %param.26) | copy-start | bytes 6148
  7.2 27.7 %all-gather.8.cloned.1.call-start = ((), (), s32[]{:S(2)}) async-start(), calls=%async_computation.5 | async-start | bytes 2621440 | tf_op jit(solution)/shard_map/all_gather | solution.py:122
  8.0 28.9 %copy-start.26 = (bf16[1024]{0:T(1024)(128)(2,1)S(1)}, bf16[1024]{0:T(1024)(128)(2,1)}, u32[]{:S(2)}) copy-start(bf16[1024]{0:T(1024)(128)(2,1)} %param.39) | copy-start | bytes 6148
  8.0 51.1 %copy-start.13 = (bf16[512,1024]{1,0:T(8,128)(2,1)S(1)}, bf16[512,1024]{1,0:T(8,128)(2,1)}, u32[]{:S(2)}) copy-start(bf16[512,1024]{1,0:T(8,128)(2,1)} %param.25) | copy-start | bytes 3145732
  8.0 51.1 %all-gather.12.cloned.1.call-start = ((), (), s32[]{:S(2)}) async-start(), calls=%async_computation.7 | async-start | bytes 2621440 | tf_op jit(solution)/shard_map/all_gather | solution.py:119
  8.7 74.5 %all-gather.10.cloned.1.call-start = ((), (), s32[]{:S(2)}) async-start(), calls=%async_computation.6 | async-start | bytes 2621440 | tf_op jit(solution)/shard_map/all_gather | solution.py:118
  9.5 97.8 %all-gather.14.cloned.1.call-start = ((), (), s32[]{:S(2)}) async-start(), calls=%async_computation.8 | async-start | bytes 2621440 | tf_op jit(solution)/shard_map/all_gather | solution.py:120
  10.0 178.0 %all-gather.16.cloned.1.call-start = ((), (), s32[]{:S(2)}) async-start(), calls=%async_computation.9 | async-start | bytes 2621440 | tf_op jit(solution)/shard_map/all_gather | solution.py:121
  10.6 208.7 %all-gather.18.cloned.1.call-start = ((), (), s32[]{:S(2)}) async-start(), calls=%async_computation.10 | async-start | bytes 10485760 | tf_op jit(solution)/shard_map/all_gather | solution.py:123
  11.2 266.9 %all-gather.20.cloned.1.call-start = ((), (), s32[]{:S(2)}) async-start(), calls=%async_computation.11 | async-start | bytes 10485760 | tf_op jit(solution)/shard_map/all_gather | solution.py:124
  36.9 177.2 %copy-start.15 = (f32[1024]{0:T(1024)}, f32[1024]{0:T(1024)S(1)}, u32[]{:S(2)}) copy-start(f32[1024]{0:T(1024)S(1)} %convert_add_fusion.1) | copy-start | bytes 12292
  112.0 4.5 collective-permute-start
  112.2 32.0 %collective-permute-start.1 = (bf16[1,512,3,256]{3,1,2,0:T(8,128)(2,1)}, bf16[1,512,3,256]{3,1,2,0:T(8,128)(2,1)}, u32[]{:S(2)}, u32[]{:S(2)}) collective-permute-start(bf16[1,512,3,256]{3,1,2,0:T(8,128)(2,1)} %get-tuple-element.230), channel_id=1, source_target_pairs={{0,2},{1,3},{2,0},{3,1},{4,6},{5,7},{6,4},{7,5},{8,10},{9,11},{10,... | collective-permute-start | bytes 2359304 | tf_op jit(solution)/shard_map/ppermute | solution.py:165
  112.7 51.0 %collective-permute-start.2 = (bf16[1,512,3,256]{3,1,2,0:T(8,128)(2,1)}, bf16[1,512,3,256]{3,1,2,0:T(8,128)(2,1)}, u32[]{:S(2)}, u32[]{:S(2)}) collective-permute-start(bf16[1,512,3,256]{3,1,2,0:T(8,128)(2,1)} %get-tuple-element.229), channel_id=1, source_target_pairs={{0,3},{1,2},{2,1},{3,0},{4,7},{5,6},{6,5},{7,4},{8,11},{9,10},{10,... | collective-permute-start | bytes 2359304 | tf_op jit(solution)/shard_map/ppermute | solution.py:165
  167.2 20.7 %copy-start.29 = (bf16[1024]{0:T(1024)(128)(2,1)S(1)}, bf16[1024]{0:T(1024)(128)(2,1)}, u32[]{:S(2)}) copy-start(bf16[1024]{0:T(1024)(128)(2,1)} %param.43) | copy-start | bytes 6148
  167.2 20.7 %copy-start.23 = (bf16[4096]{0:T(1024)(128)(2,1)S(1)}, bf16[4096]{0:T(1024)(128)(2,1)}, u32[]{:S(2)}) copy-start(bf16[4096]{0:T(1024)(128)(2,1)} %param.40) | copy-start | bytes 24580
  167.2 20.7 %copy-start.30 = (bf16[1024]{0:T(1024)(128)(2,1)S(1)}, bf16[1024]{0:T(1024)(128)(2,1)}, u32[]{:S(2)}) copy-start(bf16[1024]{0:T(1024)(128)(2,1)} %param.41) | copy-start | bytes 6148
  167.2 20.7 %copy-start.31 = (bf16[1024]{0:T(1024)(128)(2,1)S(1)}, bf16[1024]{0:T(1024)(128)(2,1)}, u32[]{:S(2)}) copy-start(bf16[1024]{0:T(1024)(128)(2,1)} %param.44) | copy-start | bytes 6148
  167.2 20.7 %copy-start.32 = (bf16[1024]{0:T(1024)(128)(2,1)S(1)}, bf16[1024]{0:T(1024)(128)(2,1)}, u32[]{:S(2)}) copy-start(bf16[1024]{0:T(1024)(128)(2,1)} %param.45) | copy-start | bytes 6148
  183.5 30.6 %all-to-all-start = ((bf16[4,512,256]{1,2,0:T(8,128)(2,1)}), bf16[4,512,256]{1,2,0:T(8,128)(2,1)}, u32[]{:S(2)}, u32[]{:S(2)}) async-start(bf16[4,512,256]{1,2,0:T(8,128)(2,1)} %get-tuple-element.79), calls=%async_computation | async-start | bytes 2097152 | tf_op jit(solution)/shard_map/all_to_all | solution.py:169
  187.8 339.4 %reduce-scatter.5.cloned.1.call-start = ((), (), s32[]{:S(2)}) async-start(), calls=%async_computation.13 | async-start | bytes 20971520 | tf_op jit(solution)/shard_map/reduce_scatter | solution.py:232
  447.0 57.1 %all-to-all-start.2 = ((bf16[4,512,3,256]{1,3,2,0:T(8,128)(2,1)}), bf16[4,512,3,256]{1,3,2,0:T(8,128)(2,1)S(1)}, u32[]{:S(2)}, u32[]{:S(2)}) async-start(bf16[4,512,3,256]{1,3,2,0:T(8,128)(2,1)} %get-tuple-element.81), calls=%async_computation.2 | async-start | bytes 6291456 | tf_op jit(solution)/shard_map/all_to_all | solution.py:211
  450.9 161.6 %reduce-scatter.3.cloned.1.call-start = ((), (), s32[]{:S(2)}) async-start(), calls=%async_computation.12 | async-start | bytes 13107200 | tf_op jit(solution)/shard_map/reduce_scatter | solution.py:244
  527.1 472.8 %all-reduce.5.cloned.1.call-start = ((), (), s32[]{:S(2)}) async-start(), calls=%async_computation.14 | async-start | bytes 16777216 | tf_op jit(solution)/shard_map/psum | solution.py:250
  (30 other events, 158.0 us)
Sparse Core Ops, SparseCore 0:
  9.6 25.2 all-gather.7
  36.5 22.5 all-gather.11
  60.6 22.5 all-gather.9
  84.6 22.5 all-gather.13
  108.6 33.8 all-gather.15
  144.0 74.2 all-gather.17
  219.8 58.2 all-gather.19
  335.8 152.4 reduce-scatter.4
  527.2 85.2 reduce-scatter.2
  617.6 382.2 all-reduce.4
